TPU v7x, 256 devices: a whole 4x4x8 slice. The times are simulated.
256 devices in a mesh: tm: 32 (over x, y, core), neur: 8 (over z).
Axes of the slice: x: 4, y: 4, z: 8, core: 2. Of those that a mesh axis runs over, the one named last changes fastest.
Arguments:
- activity: bfloat16 [51200, 12288], P('neur', 'tm'), may hold values from 0.01 to 1001, as said below
- patterns: bfloat16 [51200, 512], P('neur'), may hold values from 6.25e-05 to 0.08125, as said below
- loadings: bfloat16 [32, 12288], P(None, 'tm'), may hold values from 0.01 to 4.4, as said below
Outputs:
- h_next: float32 [32, 12288], P(None, 'tm')
- w_next: float32 [51200, 512], P(('neur', 'tm'))
- misfit: float32 [12288], P('tm')
Inputs may be any that keep to these rules, and one draw needn't show every extreme that they name: `activity`: positive. `patterns`: positive. `loadings`: positive.
All inputs are finite; a program needn't handle non-finite values.
Results may differ from a plain program's by a relative error of at most 0.0009.
Values may be sent and summed in bfloat16 or wider, within the bound.
A program may use at most 128 MiB of HBM per device.

v0:
```python
import jax
import jax.numpy as jnp
from jax import lax
from jax.sharding import PartitionSpec as P

RANK = 32
LAGS = 16


def passed_along(value, axis, steps):
    count = lax.axis_size(axis)
    leading, last = (max(0, -steps), min(count, count - steps))
    return lax.ppermute(value, axis, [(source, source + steps) for source in range(leading, last)])


def lag_stack(factor, rim):
    extended = jnp.concatenate([rim, factor], axis=1)
    width = factor.shape[1]
    rows = [extended[:, LAGS - 1 - lag : LAGS - 1 - lag + width] for lag in range(LAGS)]
    return jnp.concatenate(rows, axis=0)


def body(activity, patterns, loadings):
    span = loadings.shape[1]
    local_rows = patterns.shape[0]
    rim = passed_along(loadings[:, span - (LAGS - 1) :], "tm", 1)
    stacked = lag_stack(loadings, rim)
    recon = jnp.dot(patterns, stacked, preferred_element_type=jnp.float32)
    ratio = (activity.astype(jnp.float32) / recon).astype(jnp.bfloat16)
    ratio_next = passed_along(ratio[:, : LAGS - 1], "tm", -1)
    extended = jnp.concatenate([ratio, ratio_next], axis=1)
    gram = lax.dot_general(
        patterns, extended, (((0,), (0,)), ((), ())), preferred_element_type=jnp.float32
    )
    layered = gram.reshape(LAGS, RANK, span + LAGS - 1)
    numer = layered[0, :, 0:span]
    for lag in range(1, LAGS):
        numer = numer + layered[lag, :, lag : lag + span]
    colsum = jnp.sum(jnp.sum(patterns, axis=0, dtype=jnp.float32).reshape(LAGS, RANK), axis=0)
    numer_all, colsum_all = lax.psum((numer, colsum), "neur")
    h_next = loadings.astype(jnp.float32) * numer_all / colsum_all[:, None]
    fresh = h_next.astype(jnp.bfloat16)
    fresh_prev = passed_along(fresh[:, span - (LAGS - 1) :], "tm", 1)
    stacked_new = lag_stack(fresh, fresh_prev)
    act_wide = activity.astype(jnp.float32)
    recon_new = jnp.dot(patterns, stacked_new, preferred_element_type=jnp.float32)
    diverge = jnp.sum(act_wide * jnp.log(act_wide / recon_new) - act_wide + recon_new, axis=0)
    mass = jnp.sum(act_wide, axis=0)
    ratio_new = (act_wide / recon_new).astype(jnp.bfloat16)
    diverge_all, mass_all = lax.psum((diverge, mass), "neur")
    misfit = diverge_all / mass_all
    own_count = local_rows // lax.axis_size("tm")
    lag_part = jnp.sum(stacked_new, axis=1, dtype=jnp.float32)
    lagsum = lax.psum(lag_part, "tm")
    pnum = lax.psum_scatter(
        lax.dot_general(
            ratio_new, stacked_new, (((1,), (1,)), ((), ())), preferred_element_type=jnp.float32
        ),
        "tm",
        scatter_dimension=0,
        tiled=True,
    )
    own_patterns = lax.dynamic_slice_in_dim(
        patterns, lax.axis_index("tm") * own_count, own_count, 0
    )
    w_next = own_patterns.astype(jnp.float32) * pnum / lagsum[None, :]
    return (h_next, w_next, misfit)


def solution(mesh):
    return jax.shard_map(
        body,
        mesh=mesh,
        in_specs=(P("neur", "tm"), P("neur", None), P(None, "tm")),
        out_specs=(P(None, "tm"), P(("neur", "tm"), None), P("tm")),
        check_vma=False,
    )
```

profile of v0, /device:TPU:1, one launch (start us, length us, event | category | flops | bytes accessed | tf_op | source)
XLA Modules:
  0.0 218.1 jit_solution(12868446539411816418)
XLA Ops:
  7.2 0.8 slice.147
  8.0 4.6 %collective-permute-start = (bf16[32,15]{1,0:T(8,128)(2,1)S(1)}, bf16[32,15]{1,0:T(8,128)(2,1)S(1)}, u32[]{:S(2)}, u32[]{:S(2)}) collective-permute-start(bf16[32,15]{1,0:T(8,128)(2,1)S(1)} %slice.147), channel_id=1, source_target_pairs={{0,8},{8,16},{16,24},{24,32},{32,40},{40,48},{48,56},{56,64},{64,7... | collective-permute-start | bytes 2888 | tf_op jit(solution)/shard_map/ppermute | solution.py:13
  12.6 0.7 constant_dynamic-update-slice_fusion.15
  13.3 7.5 %copy.25 = bf16[6400,384]{0,1:T(8,128)(2,1)} copy(bf16[6400,384]{1,0:T(8,128)(2,1)} %param.3) | data formatting | bytes 9830400 | tf_op args[0]
  22.2 7.8 %fusion = bf16[6400,384]{0,1:T(8,128)(2,1)S(1)} fusion(bf16[6400,384]{0,1:T(8,128)(2,1)} %copy.25, bf16[512,384]{1,0:T(8,128)(2,1)S(1)} %constant_dynamic-update-slice_fusion, bf16[6400,512]{1,0:T(8,128)(2,1)} %param.4), kind=kOutput, calls=%fused_computation.8 | convolution fusion | flops 2523955200 | bytes 16777216 | tf_op jit(solution)/shard_map/dot_general | solution.py:28
  30.0 1.9 collective-permute-start.1
  31.9 0.3 copy-done.1
  32.2 0.9 convert_reduce_fusion.1
  33.2 3.8 %collective-permute-done.1 = bf16[6400,15]{0,1:T(8,128)(2,1)S(1)} collective-permute-done((bf16[6400,15]{0,1:T(8,128)(2,1)S(1)}, bf16[6400,15]{0,1:T(8,128)(2,1)S(1)}, u32[]{:S(2)}, u32[]{:S(2)}) %collective-permute-start.1) | collective-permute-done | bytes 192032 | tf_op jit(solution)/shard_map/ppermute | solution.py:13
  37.1 6.8 %fusion.9 = f32[512,399]{0,1:T(8,128)S(1)} fusion(bf16[6400,512]{1,0:T(8,128)(2,1)} %param.4, bf16[6400,15]{0,1:T(8,128)(2,1)S(1)} %collective-permute-done.1, bf16[6400,384]{0,1:T(8,128)(2,1)} %copy-done.1), kind=kOutput, calls=%fused_computation.17 | convolution fusion | flops 2625100800 | bytes 12477952 | tf_op jit(solution)/shard_map/dot_general | solution.py:32
  43.9 0.3 copy.26
  44.2 0.3 fusion.12
  44.5 26.0 %all-reduce.1 = (f32[32,384]{1,0:T(8,128)S(1)}, f32[32]{0:T(128)S(1)}) all-reduce(f32[32,384]{1,0:T(8,128)S(1)} %fusion.12, f32[32]{0:T(128)S(1)} %reduce_sum.46), channel_id=1, replica_groups=mesh['tm'=32,'neur'=8] {'neur'}, use_global_device_ids=true, to_apply=%region_0.0 | all-reduce | flops 12320 | bytes 98560 | tf_op jit(solution)/shard_map/psum | solution.py:40
  70.5 0.7 constant_dynamic-update-slice_fusion.31
  71.3 9.2 %collective-permute-start.2 = (bf16[32,15]{1,0:T(8,128)(2,1)S(1)}, bf16[32,15]{1,0:T(8,128)(2,1)S(1)}, u32[]{:S(2)}, u32[]{:S(2)}) collective-permute-start(bf16[32,15]{1,0:T(8,128)(2,1)S(1)} %slice.241), channel_id=1, source_target_pairs={{0,8},{8,16},{16,24},{24,32},{32,40},{40,48},{48,56},{56,64},{64,7... | collective-permute-start | bytes 2888 | tf_op jit(solution)/shard_map/ppermute | solution.py:13
  80.5 0.6 collective-permute-done.2
  82.4 7.6 %convert_reduce_fusion = (f32[384]{0:T(512)S(1)}, f32[384]{0:T(512)S(1)}, f32[6400,384]{0,1:T(8,128)S(1)}) fusion(bf16[6400,384]{0,1:T(8,128)(2,1)} %copy.25, bf16[512,384]{1,0:T(8,128)(2,1)S(1)} %constant_dynamic-update-slice_fusion.16, bf16[6400,512]{1,0:T(8,128)(2,1)} %param.4), kind=kOutput, calls=%fused_computation | convolution fusion | flops 2533784576 | bytes 21695488 | tf_op jit(solution)/shard_map/dot_general | solution.py:46
  90.1 6.8 %fusion.7 = f32[6400,512]{1,0:T(8,128)} fusion(bf16[512,384]{1,0:T(8,128)(2,1)S(1)} %constant_dynamic-update-slice_fusion.16, f32[6400,384]{0,1:T(8,128)S(1)} %get-tuple-element.12, bf16[6400,384]{0,1:T(8,128)(2,1)S(1)} %bitcast.20), kind=kOutput, calls=%fused_computation.15 | convolution fusion | flops 2523955200 | bytes 28246016 | tf_op jit(solution)/shard_map/dot_general | solution.py:56
  96.9 10.7 %all-reduce = (f32[384]{0:T(512)S(1)}, f32[384]{0:T(512)S(1)}) all-reduce(f32[384]{0:T(512)S(1)} %get-tuple-element.4, f32[384]{0:T(512)S(1)} %get-tuple-element.3), channel_id=1, replica_groups=mesh['tm'=32,'neur'=8] {'neur'}, use_global_device_ids=true, to_apply=%region_8.0 | all-reduce | flops 768 | bytes 6144 | tf_op jit(solution)/shard_map/psum | solution.py:50
  107.6 0.6 div.32
  108.2 0.1 convert_reduce_fusion.2
  108.3 67.6 %psum.37 = f32[512]{0:T(512)S(1)} all-reduce(f32[512]{0:T(512)S(1)} %convert_reduce_fusion.2), channel_id=1, replica_groups=mesh['tm'=32,'neur'=8] {'tm'}, use_global_device_ids=true, to_apply=%region_6.0 | all-reduce | flops 512 | bytes 4096 | tf_op jit(solution)/shard_map/psum | solution.py:54
  175.9 33.5 %reduce-scatter.2.cloned.1.call-done = f32[200,512]{1,0:T(8,128)} async-done(((f32[6400,512]{1,0:T(8,128)}), f32[200,512]{1,0:T(8,128)}) %reduce-scatter.2.cloned.1.call-update) | async-done | bytes 409616 | tf_op jit(solution)/shard_map/reduce_scatter | solution.py:55
  209.4 1.9 multiply_divide_fusion
  (50 shorter events, 2.9 us)
Async XLA Ops:
  7.2 13.7 %copy-start = (bf16[32,384]{1,0:T(8,128)(2,1)S(1)}, bf16[32,384]{1,0:T(8,128)(2,1)}, u32[]{:S(2)}) copy-start(bf16[32,384]{1,0:T(8,128)(2,1)} %param.5) | copy-start | bytes 73732
  7.2 202.2 %reduce-scatter.2.cloned.1.call-start = ((), (), s32[]{:S(2)}) async-start(), calls=%async_computation.1 | async-start | bytes 13516800 | tf_op jit(solution)/shard_map/reduce_scatter | solution.py:55
  8.0 12.8 %collective-permute-start = (bf16[32,15]{1,0:T(8,128)(2,1)S(1)}, bf16[32,15]{1,0:T(8,128)(2,1)S(1)}, u32[]{:S(2)}, u32[]{:S(2)}) collective-permute-start(bf16[32,15]{1,0:T(8,128)(2,1)S(1)} %slice.147), channel_id=1, source_target_pairs={{0,8},{8,16},{16,24},{24,32},{32,40},{40,48},{48,56},{56,64},{64,7... | collective-permute-start | bytes 2888 | tf_op jit(solution)/shard_map/ppermute | solution.py:13
  21.2 11.0 %slice-start = ((s8[6553600]{0:T(1024)(128)(4,1)}), s8[4194304]{0:T(1024)(128)(4,1)S(1)}, s32[]{:S(2)}) async-start(s8[6553600]{0:T(1024)(128)(4,1)} %bitcast.17), calls=%async_computation.2 | async-start | bytes 8388608
  22.2 10.1 %slice-start.1 = ((s8[6553600]{0:T(1024)(128)(4,1)}), s8[2359296]{0:T(1024)(128)(4,1)S(1)}, s32[]{:S(2)}) async-start(s8[6553600]{0:T(1024)(128)(4,1)} %bitcast.17), calls=%async_computation.3 | async-start | bytes 4718592
  30.0 2.2 %copy-start.1 = (bf16[6400,384]{0,1:T(8,128)(2,1)}, bf16[6400,384]{0,1:T(8,128)(2,1)S(1)}, u32[]{:S(2)}) copy-start(bf16[6400,384]{0,1:T(8,128)(2,1)S(1)} %fusion) | copy-start | bytes 14745604
  30.0 7.1 %collective-permute-start.1 = (bf16[6400,15]{0,1:T(8,128)(2,1)S(1)}, bf16[6400,15]{0,1:T(8,128)(2,1)S(1)}, u32[]{:S(2)}, u32[]{:S(2)}) collective-permute-start(bf16[6400,15]{0,1:T(8,128)(2,1)S(1)} %slice.224), channel_id=1, source_target_pairs={{8,0},{16,8},{24,16},{32,24},{40,32},{48,40},{56,48},{64,56},{72,6... | collective-permute-start | bytes 576008 | tf_op jit(solution)/shard_map/ppermute | solution.py:13
  44.2 45.8 %slice-start.2 = ((s8[4915200]{0:T(1024)(128)(4,1)}), s8[720896]{0:T(1024)(128)(4,1)S(1)}, s32[]{:S(2)}) async-start(s8[4915200]{0:T(1024)(128)(4,1)} %bitcast.19), calls=%async_computation.4 | async-start | bytes 1441792
  71.3 9.8 %collective-permute-start.2 = (bf16[32,15]{1,0:T(8,128)(2,1)S(1)}, bf16[32,15]{1,0:T(8,128)(2,1)S(1)}, u32[]{:S(2)}, u32[]{:S(2)}) collective-permute-start(bf16[32,15]{1,0:T(8,128)(2,1)S(1)} %slice.241), channel_id=1, source_target_pairs={{0,8},{8,16},{16,24},{24,32},{32,40},{40,48},{48,56},{56,64},{64,7... | collective-permute-start | bytes 2888 | tf_op jit(solution)/shard_map/ppermute | solution.py:13
  82.4 7.7 %slice-start.3 = ((s8[4915200]{0:T(1024)(128)(4,1)}), s8[4194304]{0:T(1024)(128)(4,1)S(1)}, s32[]{:S(2)}) async-start(s8[4915200]{0:T(1024)(128)(4,1)} %bitcast.19), calls=%async_computation.5 | async-start | bytes 8388608
Sparse Core Ops, SparseCore 0:
  97.0 112.3 reduce-scatter.1
where the time goes:
time: 219 us; the launch traced here: 218 us
  blocking collectives  104 us (47%)
  waiting for transfers between devices  38 us (17%)
  matrix products  29 us (13%)
  starting transfers between devices  15.8 us (7%)
  between operations  14.2 us (6%)
  local copies, waits for them, and re-layouts  9.82 us (4%)
  other arithmetic  7.12 us (3%)
    psum x1, blocking collectives, body(): lagsum = lax.psum(lag_part, 'tm')  67.6 us
    reduce_scatter x1, waiting for transfers between devices, body(): lax.psum_scatter(lax.dot_general(ratio_new, stacked_new, (((1,), (1,)), (...  33.5 us
    psum x1, blocking collectives, body(): numer_all, colsum_all = lax.psum((numer, colsum), 'neur')  26 us
    ppermute x3, starting transfers between devices, passed_along(): lax.ppermute(value, axis, [(source, source + steps) for source in range(l...  15.7 us
    psum x1, blocking collectives, body(): diverge_all, mass_all = lax.psum((diverge, mass), 'neur')  10.7 us
    unnamed x14, local copies, waits for them, and re-layouts  8.53 us
    dot_general x1, matrix products, body(): recon = jnp.dot(patterns, stacked, preferred_element_type=jnp.float32)  7.79 us
    dot_general x1, matrix products, body(): jnp.dot(patterns, stacked_new, preferred_element_type=jnp.float32)  7.64 us
  transfers between devices with their start and end apart: 4, of which 3 were waited for; matrix products, arithmetic and copies ran while one was open for 5% of the time, Pallas kernels for 0%

commit v1 on v0

--- a/solution.py
+++ b/solution.py
@@ -51,7 +51,7 @@
     misfit = diverge_all / mass_all
     own_count = local_rows // lax.axis_size("tm")
     lag_part = jnp.sum(stacked_new, axis=1, dtype=jnp.float32)
-    lagsum = lax.psum(lag_part, "tm")
+    lagsum = jnp.sum(lax.all_gather(lag_part, "tm"), axis=0)
     pnum = lax.psum_scatter(
         lax.dot_general(
             ratio_new, stacked_new, (((1,), (1,)), ((), ())), preferred_element_type=jnp.float32

time: 219 us -> 219 us (level)
  waiting for transfers between devices: 38 us -> 76.6 us
  blocking collectives: 104 us -> 65.6 us
    psum x1 -> x0, blocking collectives: 67.6 us -> none  [body(): lagsum = lax.psum(lag_part, 'tm')]
    reduce_scatter x1, waiting for transfers between devices: 33.5 us -> 72.1 us  [body(): lax.psum_scatter(lax.dot_general(ratio_new, stacked_new, (((1,), (1,)), (...]
    all_gather x0 -> x1, blocking collectives: none -> 28.9 us  [body(): lagsum = jnp.sum(lax.all_gather(lag_part, 'tm'), axis=0)]
where the time goes in v1:
time: 219 us; the launch traced here: 218 us
  waiting for transfers between devices  76.6 us (35%)
  blocking collectives  65.6 us (30%)
  matrix products  29 us (13%)
  starting transfers between devices  15.8 us (7%)
  between operations  14.2 us (6%)
  local copies, waits for them, and re-layouts  9.82 us (4%)
  other arithmetic  7.19 us (3%)
    reduce_scatter x1, waiting for transfers between devices, body(): lax.psum_scatter(lax.dot_general(ratio_new, stacked_new, (((1,), (1,)), (...  72.1 us
    all_gather x1, blocking collectives, body(): lagsum = jnp.sum(lax.all_gather(lag_part, 'tm'), axis=0)  28.9 us
    psum x1, blocking collectives, body(): numer_all, colsum_all = lax.psum((numer, colsum), 'neur')  26 us
    ppermute x3, starting transfers between devices, passed_along(): lax.ppermute(value, axis, [(source, source + steps) for source in range(l...  15.7 us
    psum x1, blocking collectives, body(): diverge_all, mass_all = lax.psum((diverge, mass), 'neur')  10.7 us
    unnamed x14, local copies, waits for them, and re-layouts  8.53 us
    dot_general x1, matrix products, body(): recon = jnp.dot(patterns, stacked, preferred_element_type=jnp.float32)  7.79 us
    dot_general x1, matrix products, body(): jnp.dot(patterns, stacked_new, preferred_element_type=jnp.float32)  7.72 us
  transfers between devices with their start and end apart: 4, of which 3 were waited for; matrix products, arithmetic and copies ran while one was open for 5% of the time, Pallas kernels for 0%

profile of v1, /device:TPU:1, one launch (start us, length us, event | category | flops | bytes accessed | tf_op | source)
XLA Modules:
  0.0 218.2 jit_solution(2674022671627347716)
XLA Ops:
  7.2 0.8 slice.147
  8.0 4.6 %collective-permute-start = (bf16[32,15]{1,0:T(8,128)(2,1)S(1)}, bf16[32,15]{1,0:T(8,128)(2,1)S(1)}, u32[]{:S(2)}, u32[]{:S(2)}) collective-permute-start(bf16[32,15]{1,0:T(8,128)(2,1)S(1)} %slice.147), channel_id=1, source_target_pairs={{0,8},{8,16},{16,24},{24,32},{32,40},{40,48},{48,56},{56,64},{64,7... | collective-permute-start | bytes 2888 | tf_op jit(solution)/shard_map/ppermute | solution.py:13
  12.6 0.7 constant_dynamic-update-slice_fusion.15
  13.3 7.5 %copy.27 = bf16[6400,384]{0,1:T(8,128)(2,1)} copy(bf16[6400,384]{1,0:T(8,128)(2,1)} %param.3) | data formatting | bytes 9830400 | tf_op args[0]
  22.2 7.8 %fusion = bf16[6400,384]{0,1:T(8,128)(2,1)S(1)} fusion(bf16[6400,384]{0,1:T(8,128)(2,1)} %copy.27, bf16[512,384]{1,0:T(8,128)(2,1)S(1)} %constant_dynamic-update-slice_fusion, bf16[6400,512]{1,0:T(8,128)(2,1)} %param.4), kind=kOutput, calls=%fused_computation.8 | convolution fusion | flops 2523955200 | bytes 16777216 | tf_op jit(solution)/shard_map/dot_general | solution.py:28
  30.0 1.9 collective-permute-start.1
  31.9 0.3 copy-done.1
  32.2 0.9 convert_reduce_fusion.1
  33.2 3.8 %collective-permute-done.1 = bf16[6400,15]{0,1:T(8,128)(2,1)S(1)} collective-permute-done((bf16[6400,15]{0,1:T(8,128)(2,1)S(1)}, bf16[6400,15]{0,1:T(8,128)(2,1)S(1)}, u32[]{:S(2)}, u32[]{:S(2)}) %collective-permute-start.1) | collective-permute-done | bytes 192032 | tf_op jit(solution)/shard_map/ppermute | solution.py:13
  37.1 6.8 %fusion.9 = f32[512,399]{0,1:T(8,128)S(1)} fusion(bf16[6400,512]{1,0:T(8,128)(2,1)} %param.4, bf16[6400,15]{0,1:T(8,128)(2,1)S(1)} %collective-permute-done.1, bf16[6400,384]{0,1:T(8,128)(2,1)} %copy-done.1), kind=kOutput, calls=%fused_computation.17 | convolution fusion | flops 2625100800 | bytes 12477952 | tf_op jit(solution)/shard_map/dot_general | solution.py:32
  43.9 0.3 copy.28
  44.2 0.3 fusion.12
  44.5 26.0 %all-reduce.1 = (f32[32,384]{1,0:T(8,128)S(1)}, f32[32]{0:T(128)S(1)}) all-reduce(f32[32,384]{1,0:T(8,128)S(1)} %fusion.12, f32[32]{0:T(128)S(1)} %reduce_sum.55), channel_id=1, replica_groups=mesh['tm'=32,'neur'=8] {'neur'}, use_global_device_ids=true, to_apply=%region_0.0 | all-reduce | flops 12320 | bytes 98560 | tf_op jit(solution)/shard_map/psum | solution.py:40
  70.5 0.7 constant_dynamic-update-slice_fusion.31
  71.2 9.2 %collective-permute-start.2 = (bf16[32,15]{1,0:T(8,128)(2,1)S(1)}, bf16[32,15]{1,0:T(8,128)(2,1)S(1)}, u32[]{:S(2)}, u32[]{:S(2)}) collective-permute-start(bf16[32,15]{1,0:T(8,128)(2,1)S(1)} %slice.241), channel_id=1, source_target_pairs={{0,8},{8,16},{16,24},{24,32},{32,40},{40,48},{48,56},{56,64},{64,7... | collective-permute-start | bytes 2888 | tf_op jit(solution)/shard_map/ppermute | solution.py:13
  80.5 0.6 collective-permute-done.2
  82.4 7.7 %convert_reduce_fusion = (f32[384]{0:T(512)S(1)}, f32[384]{0:T(512)S(1)}, f32[6400,384]{0,1:T(8,128)S(1)}) fusion(bf16[6400,384]{0,1:T(8,128)(2,1)} %copy.27, bf16[512,384]{1,0:T(8,128)(2,1)S(1)} %constant_dynamic-update-slice_fusion.16, bf16[6400,512]{1,0:T(8,128)(2,1)} %param.4), kind=kOutput, calls=%fused_computation | convolution fusion | flops 2533784576 | bytes 21695488 | tf_op jit(solution)/shard_map/dot_general | solution.py:46
  90.1 6.8 %fusion.7 = f32[6400,512]{1,0:T(8,128)} fusion(bf16[512,384]{1,0:T(8,128)(2,1)S(1)} %constant_dynamic-update-slice_fusion.16, f32[6400,384]{0,1:T(8,128)S(1)} %get-tuple-element.12, bf16[6400,384]{0,1:T(8,128)(2,1)S(1)} %bitcast.21), kind=kOutput, calls=%fused_computation.15 | convolution fusion | flops 2523955200 | bytes 28246016 | tf_op jit(solution)/shard_map/dot_general | solution.py:56
  96.9 0.1 convert_reduce_fusion.2
  97.1 28.9 %all-gather.1 = f32[32,1,512]{2,1,0:T(1,128)S(1)} all-gather(f32[1,1,512]{2,1,0:T(1,128)S(1)} %bitcast.23), channel_id=2, replica_groups=mesh['tm'=32,'neur'=8] {'tm'}, dimensions={0}, use_global_device_ids=true | all-gather | bytes 67584 | tf_op jit(solution)/shard_map/all_gather | solution.py:54
  126.1 10.7 %all-reduce = (f32[384]{0:T(512)S(1)}, f32[384]{0:T(512)S(1)}) all-reduce(f32[384]{0:T(512)S(1)} %get-tuple-element.4, f32[384]{0:T(512)S(1)} %get-tuple-element.3), channel_id=1, replica_groups=mesh['tm'=32,'neur'=8] {'neur'}, use_global_device_ids=true, to_apply=%region_8.0 | all-reduce | flops 768 | bytes 6144 | tf_op jit(solution)/shard_map/psum | solution.py:50
  136.8 0.6 div.32
  137.4 72.1 %reduce-scatter.2.cloned.1.call-done = f32[200,512]{1,0:T(8,128)} async-done(((f32[6400,512]{1,0:T(8,128)}), f32[200,512]{1,0:T(8,128)}) %reduce-scatter.2.cloned.1.call-update) | async-done | bytes 409616 | tf_op jit(solution)/shard_map/reduce_scatter | solution.py:55
  209.5 1.9 multiply_divide_fusion
  (51 shorter events, 3.0 us)
Async XLA Ops:
  7.2 13.7 %copy-start = (bf16[32,384]{1,0:T(8,128)(2,1)S(1)}, bf16[32,384]{1,0:T(8,128)(2,1)}, u32[]{:S(2)}) copy-start(bf16[32,384]{1,0:T(8,128)(2,1)} %param.5) | copy-start | bytes 73732
  7.2 202.3 %reduce-scatter.2.cloned.1.call-start = ((), (), s32[]{:S(2)}) async-start(), calls=%async_computation.1 | async-start | bytes 13516800 | tf_op jit(solution)/shard_map/reduce_scatter | solution.py:55
  8.0 12.8 %collective-permute-start = (bf16[32,15]{1,0:T(8,128)(2,1)S(1)}, bf16[32,15]{1,0:T(8,128)(2,1)S(1)}, u32[]{:S(2)}, u32[]{:S(2)}) collective-permute-start(bf16[32,15]{1,0:T(8,128)(2,1)S(1)} %slice.147), channel_id=1, source_target_pairs={{0,8},{8,16},{16,24},{24,32},{32,40},{40,48},{48,56},{56,64},{64,7... | collective-permute-start | bytes 2888 | tf_op jit(solution)/shard_map/ppermute | solution.py:13
  21.2 11.0 %slice-start = ((s8[6553600]{0:T(1024)(128)(4,1)}), s8[4194304]{0:T(1024)(128)(4,1)S(1)}, s32[]{:S(2)}) async-start(s8[6553600]{0:T(1024)(128)(4,1)} %bitcast.18), calls=%async_computation.2 | async-start | bytes 8388608
  22.2 10.1 %slice-start.1 = ((s8[6553600]{0:T(1024)(128)(4,1)}), s8[2359296]{0:T(1024)(128)(4,1)S(1)}, s32[]{:S(2)}) async-start(s8[6553600]{0:T(1024)(128)(4,1)} %bitcast.18), calls=%async_computation.3 | async-start | bytes 4718592
  30.0 2.2 %copy-start.1 = (bf16[6400,384]{0,1:T(8,128)(2,1)}, bf16[6400,384]{0,1:T(8,128)(2,1)S(1)}, u32[]{:S(2)}) copy-start(bf16[6400,384]{0,1:T(8,128)(2,1)S(1)} %fusion) | copy-start | bytes 14745604
  30.0 7.1 %collective-permute-start.1 = (bf16[6400,15]{0,1:T(8,128)(2,1)S(1)}, bf16[6400,15]{0,1:T(8,128)(2,1)S(1)}, u32[]{:S(2)}, u32[]{:S(2)}) collective-permute-start(bf16[6400,15]{0,1:T(8,128)(2,1)S(1)} %slice.224), channel_id=1, source_target_pairs={{8,0},{16,8},{24,16},{32,24},{40,32},{48,40},{56,48},{64,56},{72,6... | collective-permute-start | bytes 576008 | tf_op jit(solution)/shard_map/ppermute | solution.py:13
  44.2 45.9 %slice-start.2 = ((s8[4915200]{0:T(1024)(128)(4,1)}), s8[720896]{0:T(1024)(128)(4,1)S(1)}, s32[]{:S(2)}) async-start(s8[4915200]{0:T(1024)(128)(4,1)} %bitcast.20), calls=%async_computation.4 | async-start | bytes 1441792
  71.2 9.8 %collective-permute-start.2 = (bf16[32,15]{1,0:T(8,128)(2,1)S(1)}, bf16[32,15]{1,0:T(8,128)(2,1)S(1)}, u32[]{:S(2)}, u32[]{:S(2)}) collective-permute-start(bf16[32,15]{1,0:T(8,128)(2,1)S(1)} %slice.241), channel_id=1, source_target_pairs={{0,8},{8,16},{16,24},{24,32},{32,40},{40,48},{48,56},{56,64},{64,7... | collective-permute-start | bytes 2888 | tf_op jit(solution)/shard_map/ppermute | solution.py:13
  82.4 7.7 %slice-start.3 = ((s8[4915200]{0:T(1024)(128)(4,1)}), s8[4194304]{0:T(1024)(128)(4,1)S(1)}, s32[]{:S(2)}) async-start(s8[4915200]{0:T(1024)(128)(4,1)} %bitcast.20), calls=%async_computation.5 | async-start | bytes 8388608
Sparse Core Ops, SparseCore 0:
  97.0 112.3 reduce-scatter.1
